TPU v7x, 256 devices: a whole 4x4x8 slice. The times are simulated.
256 devices in a mesh: band: 8 (over x_lo, y), dev: 32 (over x_hi, z, core).
Axes of the slice: x: 4 (x_hi: 2, x_lo: 2; x = x_hi * 2 + x_lo), y: 4, z: 8, core: 2. Of those that a mesh axis runs over, the one named last changes fastest.
Arguments:
- drive: float32 [2, 32, 131072], P(None, None, ('band', 'dev')), may hold values from -6 to 6
- coords: float32 [3, 131072], P(None, ('band', 'dev')), may hold values from 0 to 3
- rule_index: int32 [131072], P(('band', 'dev')), may hold values from 0 to 3
- rule_weight: float32 [4], replicated, may hold values from 0.1 to 0.4
- pair_cols: int32 [24576], P(('band', 'dev')), may hold values from 0 to 511, as said below
- pair_count: int32 [256], P(('band', 'dev')), may hold values from 12 to 96, as said below
Outputs:
- near_field: float32 [2, 32, 131072], P(None, None, ('band', 'dev'))
Inputs may be any that keep to these rules, and one draw needn't show every extreme that they name: `pair_cols`: for slot s of device k the listed block column lies from k * 2 + (s mod 2) up to that row plus 64 - 1; slots s < 2 list the diagonal pair. `pair_count`: some device has all 96 slots live.
All inputs are finite; a program needn't handle non-finite values.
Results may differ from a plain program's by a relative error of at most 0.0003.
Values sent between devices are 32-bit elements; how exact they have to be, the bound alone decides.
A program may use at most 64 MiB of HBM per device.

v0:
```python
import math

import jax
import jax.numpy as jnp
from jax import lax
from jax.sharding import PartitionSpec as P

BLOCK = 256
RULES = 4
BR_DEV = 2
TILE_DEV = 96


wave_number = 25.0
smoothing = 0.05
highest = lax.Precision.HIGHEST


def from_behind(value, axis, steps):
    count = lax.axis_size(axis)
    initial, last = (max(0, -steps), min(count, count - steps))
    return lax.ppermute(value, axis, [(source, source + steps) for source in range(initial, last)])


def point_weights(rule_index, rule_weight):
    matches = rule_index[:, None] == jnp.arange(RULES, dtype=jnp.int32)[None, :]
    return jnp.sum(
        jnp.where(matches, rule_weight[None, :], jnp.zeros_like(rule_weight)[None, :]), axis=1
    )


def assemble(near_points, far_points, near_w, far_w):
    offsets = near_points[:, :, None] - far_points[:, None, :]
    distance = jnp.sqrt(jnp.sum(offsets * offsets, axis=0) + smoothing * smoothing)
    strength = near_w[:, None] * far_w[None, :] / (4.0 * math.pi * distance)
    phases = wave_number * distance
    return (strength * jnp.cos(phases), strength * jnp.sin(phases))


def batch_apply(vectors, real_part, imag_part, form):
    real_prod = jnp.einsum(
        form, vectors, real_part, precision=highest, preferred_element_type=jnp.float32
    )
    imag_prod = jnp.einsum(
        form, vectors, imag_part, precision=highest, preferred_element_type=jnp.float32
    )
    return jnp.stack([real_prod[:, 0] - imag_prod[:, 1], real_prod[:, 1] + imag_prod[:, 0]], axis=1)


def add_block(accumulated, update_block, block_index):
    previous = lax.dynamic_slice_in_dim(accumulated, block_index * BLOCK, BLOCK, 2)
    return lax.dynamic_update_slice_in_dim(
        accumulated, previous + update_block, block_index * BLOCK, 2
    )


def body(drive, coords, rule_index, rule_weight, pair_cols, pair_count):
    n_dev = lax.axis_size("dev")
    band_index = lax.axis_index("band")
    dev_index = lax.axis_index("dev")
    patterns = drive.shape[1]
    own_cols = drive.shape[2]
    band_cols = n_dev * own_cols
    weights = point_weights(rule_index, rule_weight)
    geometry = jnp.concatenate([coords, weights[None, :]], axis=0)
    band_rows = n_dev * BR_DEV
    band_first = band_index * band_rows
    band_x, band_g = (
        lax.all_gather(drive, "dev", axis=2, tiled=True),
        lax.all_gather(geometry, "dev", axis=1, tiled=True),
    )
    next_x, next_g = from_behind((band_x, band_g), "band", -1)
    window_x = jnp.concatenate([band_x, next_x], axis=2)
    window_g = jnp.concatenate([band_g, next_g], axis=1)
    local_slot = jnp.arange(TILE_DEV, dtype=jnp.int32)
    tile_rows = dev_index * BR_DEV + local_slot % BR_DEV
    tile_cols = pair_cols - band_first
    live_tiles = pair_count[0]
    per_turn = 8
    turns = (live_tiles + per_turn - 1) // per_turn

    def one_turn(turn_index, accumulated):
        first_slot = turn_index * per_turn
        pick_rows = lax.dynamic_slice_in_dim(tile_rows, first_slot, per_turn, 0)
        pick_cols = lax.dynamic_slice_in_dim(tile_cols, first_slot, per_turn, 0)
        slot_ids = first_slot + jnp.arange(per_turn, dtype=jnp.int32)
        keep_mask = (slot_ids < live_tiles).astype(jnp.float32)
        mirror = keep_mask * (pick_rows != pick_cols).astype(jnp.float32)
        near_x = jnp.stack(
            [
                lax.dynamic_slice_in_dim(window_x, pick_rows[g] * BLOCK, BLOCK, 2)
                for g in range(per_turn)
            ]
        )
        far_x = jnp.stack(
            [
                lax.dynamic_slice_in_dim(window_x, pick_cols[g] * BLOCK, BLOCK, 2)
                for g in range(per_turn)
            ]
        )
        near_g = jnp.stack(
            [
                lax.dynamic_slice_in_dim(window_g, pick_rows[g] * BLOCK, BLOCK, 1)
                for g in range(per_turn)
            ]
        )
        far_g = jnp.stack(
            [
                lax.dynamic_slice_in_dim(window_g, pick_cols[g] * BLOCK, BLOCK, 1)
                for g in range(per_turn)
            ]
        )
        real_part, imag_part = jax.vmap(assemble)(
            near_g[:, :3], far_g[:, :3], near_g[:, 3], far_g[:, 3]
        )
        direct = (
            batch_apply(far_x, real_part, imag_part, "tcrq,tpq->tcrp")
            * keep_mask[:, None, None, None]
        )
        mirrored = (
            batch_apply(near_x, real_part, imag_part, "tcrp,tpq->tcrq")
            * mirror[:, None, None, None]
        )
        for g in range(per_turn):
            accumulated = add_block(accumulated, direct[g], pick_rows[g])
            accumulated = add_block(accumulated, mirrored[g], pick_cols[g])
        return accumulated

    accumulated = jnp.zeros((2, patterns, 2 * band_cols), jnp.float32)
    accumulated = lax.fori_loop(0, turns, one_turn, accumulated)
    own_part = accumulated[:, :, :band_cols]
    next_part = accumulated[:, :, band_cols:]
    carried = from_behind(next_part, "band", 1)
    return lax.psum_scatter(own_part + carried, "dev", scatter_dimension=2, tiled=True)


def solution(mesh):
    in_specs = (
        P(None, None, ("band", "dev")),
        P(None, ("band", "dev")),
        P(("band", "dev")),
        P(),
        P(("band", "dev")),
        P(("band", "dev")),
    )
    out_specs = P(None, None, ("band", "dev"))
    return jax.shard_map(body, mesh=mesh, in_specs=in_specs, out_specs=out_specs, check_vma=False)
```

profile of v0, /device:TPU:1, one launch (start us, length us, event | category | flops | bytes accessed | tf_op | source)
XLA Modules:
  0.0 1447.4 jit_solution(17859548919248176330)
XLA Ops:
  7.3 93.7 %all-gather.2.cloned.1.call-done = f32[2,32,16384]{2,1,0:T(8,128)} async-done(((f32[2,32,512]{2,1,0:T(8,128)}), f32[2,32,16384]{2,1,0:T(8,128)}) %all-gather.2.cloned.1.call-update) | async-done | bytes 4194320 | tf_op jit(solution)/shard_map/all_gather | solution.py:69
  103.7 38.7 %all_gather.7 = f32[4,16384]{1,0:T(4,128)S(1)} all-gather(f32[4,512]{1,0:T(4,128)S(1)} %pad_maximum_fusion.2), channel_id=1, replica_groups=mesh['band'=8,'dev'=32] {'dev'}, dimensions={1}, use_global_device_ids=true | all-gather | bytes 270336 | tf_op jit(solution)/shard_map/all_gather | solution.py:70
  145.1 55.5 %collective-permute-done.1 = f32[4,16384]{1,0:T(4,128)S(1)} collective-permute-done((f32[4,16384]{1,0:T(4,128)S(1)}, f32[4,16384]{1,0:T(4,128)S(1)}, u32[]{:S(2)}, u32[]{:S(2)}) %collective-permute-start.1) | collective-permute-done | bytes 262176 | tf_op jit(solution)/shard_map/ppermute | solution.py:22
  200.7 7.3 pad_maximum_fusion
  208.0 3.9 broadcast_in_dim.20
  211.9 351.3 %while.10 = (s32[]{:T(128)}, f32[2,32,32768]{2,1,0:T(8,128)}, s32[]{:T(128)}, s32[96]{0:T(128)S(1)}, s32[96]{0:T(128)S(1)}, /*index=5*/f32[2,32,32768]{2,1,0:T(8...) while((s32[]{:T(128)}, f32[2,32,32768]{2,1,0:T(8,128)}, ...), condition=%wide.region_3.4_spmd, body=%wide.region_1.3_spmd.sunk | while | flops 1628438656 | bytes 25904608 | solution.py:130
  233.0 10.4 fusion.90
  243.4 10.6 fusion.89
  254.0 10.8 fusion.88
  264.9 10.9 fusion.87
  276.1 1.5 fusion.91
  277.6 1.5 fusion.92
  282.0 1.5 fusion.95
  287.9 1.5 fusion.99
  293.8 1.5 fusion.103
  295.3 1.5 fusion.104
  320.8 10.4 fusion.90
  331.2 10.6 fusion.89
  341.9 10.8 fusion.88
  352.7 10.9 fusion.87
  363.9 1.5 fusion.91
  369.8 1.5 fusion.95
  374.2 1.5 fusion.98
  375.7 1.5 fusion.99
  381.6 1.5 fusion.103
  408.5 10.4 fusion.90
  419.0 10.6 fusion.89
  429.6 10.8 fusion.88
  440.5 10.9 fusion.87
  451.6 1.5 fusion.91
  457.6 1.5 fusion.95
  463.5 1.5 fusion.99
  469.4 1.5 fusion.103
  496.3 10.4 fusion.90
  506.8 10.6 fusion.89
  517.4 10.8 fusion.88
  528.2 10.9 fusion.87
  539.4 1.5 fusion.91
  543.9 1.5 fusion.94
  545.4 1.5 fusion.95
  551.3 1.5 fusion.99
  555.7 1.5 fusion.102
  557.2 1.5 fusion.103
  563.2 2.6 slice.171
  565.8 3.8 collective-permute-start.2
  569.6 45.2 %collective-permute-done.2 = f32[2,32,16384]{2,1,0:T(8,128)S(1)} collective-permute-done((f32[2,32,16384]{2,1,0:T(8,128)S(1)}, f32[2,32,16384]{2,1,0:T(8,128)S(1)}, u32[]{:S(2)}, u32[]{:S(2)}) %collective-permute-start.2) | collective-permute-done | bytes 4194336 | tf_op jit(solution)/shard_map/ppermute | solution.py:22
  614.7 2.4 slice_add_fusion.2
  617.1 823.4 %reduce-scatter.2.cloned.1.call-done = f32[2,32,512]{2,1,0:T(8,128)} async-done(((f32[2,32,16384]{2,1,0:T(8,128)}), f32[2,32,512]{2,1,0:T(8,128)}) %reduce-scatter.2.cloned.1.call-update) | async-done | bytes 131088 | tf_op jit(solution)/shard_map/reduce_scatter | solution.py:134
  (216 shorter events, 112.8 us)
Async XLA Ops:
  6.5 94.4 %all-gather.2.cloned.1.call-start = ((), (), s32[]{:S(2)}) async-start(), calls=%async_computation.1 | async-start | bytes 4325376 | tf_op jit(solution)/shard_map/all_gather | solution.py:69
  7.3 1433.3 %reduce-scatter.2.cloned.1.call-start = ((), (), s32[]{:S(2)}) async-start(), calls=%async_computation.2 | async-start | bytes 4325376 | tf_op jit(solution)/shard_map/reduce_scatter | solution.py:134
  101.0 99.7 %collective-permute-start = (f32[2,32,16384]{2,1,0:T(8,128)}, f32[2,32,16384]{2,1,0:T(8,128)}, u32[]{:S(2)}, u32[]{:S(2)}) collective-permute-start(f32[2,32,16384]{2,1,0:T(8,128)} %all-gather.2.cloned.1.call-done), channel_id=1, source_target_pairs={{32,0},{64,32},{96,64},{128,96},{160,128},{192,160},{224,192},{33,... | collective-permute-start | bytes 12582920 | tf_op jit(solution)/shard_map/ppermute | solution.py:22
  142.4 58.1 %collective-permute-start.1 = (f32[4,16384]{1,0:T(4,128)S(1)}, f32[4,16384]{1,0:T(4,128)S(1)}, u32[]{:S(2)}, u32[]{:S(2)}) collective-permute-start(f32[4,16384]{1,0:T(4,128)S(1)} %all_gather.7), channel_id=1, source_target_pairs={{32,0},{64,32},{96,64},{128,96},{160,128},{192,160},{224,192},{33,... | collective-permute-start | bytes 786440 | tf_op jit(solution)/shard_map/ppermute | solution.py:22
  563.2 51.6 %copy-start = (f32[2,32,32768]{2,1,0:T(8,128)S(1)}, f32[2,32,32768]{2,1,0:T(8,128)}, u32[]{:S(2)}) copy-start(f32[2,32,32768]{2,1,0:T(8,128)} %get-tuple-element.48) | copy-start | bytes 25165828
  565.8 48.9 %collective-permute-start.2 = (f32[2,32,16384]{2,1,0:T(8,128)S(1)}, f32[2,32,16384]{2,1,0:T(8,128)S(1)}, u32[]{:S(2)}, u32[]{:S(2)}) collective-permute-start(f32[2,32,16384]{2,1,0:T(8,128)S(1)} %slice.171), channel_id=1, source_target_pairs={{0,32},{32,64},{64,96},{96,128},{128,160},{160,192},{192,224},{1,3... | collective-permute-start | bytes 12582920 | tf_op jit(solution)/shard_map/ppermute | solution.py:22
Sparse Core Ops, SparseCore 0:
  10.2 90.7 all-gather.1
  617.3 823.2 reduce-scatter.1
where the time goes:
time: 1470 us; the launch traced here: 1450 us
  waiting for transfers between devices  1020 us (69%)
  matrix products  171 us (12%)
  other arithmetic  115 us (8%)
  local copies, waits for them, and re-layouts  41.9 us (3%)
  loops' own time  41.6 us (3%)
  blocking collectives  38.7 us (3%)
    reduce_scatter x1, waiting for transfers between devices, body(): lax.psum_scatter(own_part + carried, 'dev', scatter_dimension=2, tiled=True)  823 us
    ppermute x3, waiting for transfers between devices, from_behind(): lax.ppermute(value, axis, [(source, source + steps) for source in range(i...  101 us
    dynamic_update_slice x64, other arithmetic, add_block(): lax.dynamic_update_slice_in_dim(accumulated, previous + update_block, blo...  94.8 us
    all_gather x1, waiting for transfers between devices, body(): lax.all_gather(drive, 'dev', axis=2, tiled=True)  93.7 us
    dot_general x8, matrix products, batch_apply(): jnp.einsum(form, vectors, imag_part, precision=highest, preferred_element...  86 us
    dot_general x8, matrix products, batch_apply(): jnp.einsum(form, vectors, real_part, precision=highest, preferred_element...  85.1 us
    another operation x1, loops' own time, body(): accumulated = lax.fori_loop(0, turns, one_turn, accumulated)  41.6 us
    all_gather x1, blocking collectives, body(): lax.all_gather(geometry, 'dev', axis=1, tiled=True)  38.7 us
  transfers between devices with their start and end apart: 5, of which 4 were waited for; matrix products, arithmetic and copies ran while one was open for 0% of the time, Pallas kernels for 0%

commit v1 on v0

v1 whole, which is shorter than its diff:
```python
import math, functools
import jax, jax.numpy as jnp
from jax import lax
from jax.sharding import PartitionSpec as P
from jax.experimental import pallas as pl
from jax.experimental.pallas import tpu as pltpu

BLOCK=256
TURN = 25.0 / (2.0 * math.pi)
GAIN = 25.0 / (8.0 * math.pi**2)
SMOOTH2 = (0.05*TURN)**2
SIN = (4.4428829191996, -7.308245696145797, 3.6063544112192103, -0.8461128844269574, 0.10982698484738432)
COS = (1.4142134965645703, -6.978850988181998, 5.739461169540789, -1.8835629799935238, 0.3106981771853715)
ROWS = 32

def horner(z, c):
    v = c[-1]
    for k in c[-2::-1]:
        v = v * z + k
    return v

def split(v):
    hi = v.astype(jnp.bfloat16)
    return hi, (v - hi.astype(jnp.float32)).astype(jnp.bfloat16)

def build_tile(row, col, p_ref, q_ref, hi_ref, lo_ref):
    qx = q_ref[col, 0:1, :]
    qy = q_ref[col, 1:2, :]
    qz = q_ref[col, 2:3, :]
    for r in range(0, BLOCK, ROWS):
        px = p_ref[row, 0, r:r+ROWS, :]
        py = p_ref[row, 1, r:r+ROWS, :]
        pz = p_ref[row, 2, r:r+ROWS, :]
        px = jnp.concatenate([px, px], axis=1)
        py = jnp.concatenate([py, py], axis=1)
        pz = jnp.concatenate([pz, pz], axis=1)
        dx = px - qx
        dy = py - qy
        dz = pz - qz
        d2 = dx*dx + (dy*dy + (dz*dz + SMOOTH2))
        inv = lax.rsqrt(d2)
        turns = d2 * inv
        f = turns - jnp.round(turns)
        z = f * f
        s = f * horner(z, SIN)
        c = horner(z, COS)
        t = inv * s
        re = inv - t * s
        im = t * c
        rh, rl = split(re)
        ih, il = split(im)
        hi_ref[r:r+ROWS, 0:BLOCK] = rh
        hi_ref[r:r+ROWS, BLOCK:] = ih
        lo_ref[r:r+ROWS, 0:BLOCK] = rl
        lo_ref[r:r+ROWS, BLOCK:] = il

NT = (((1,), (1,)), ((), ()))
NN = (((1,), (0,)), ((), ()))

def dotf(a, b, dims):
    return lax.dot_general(a, b, dims, preferred_element_type=jnp.float32)

def apply_tile(row, col, md, mm, li_ref, lj_ref, hi_ref, lo_ref, yi_ref, yj_ref):
    a = dotf(lj_ref[col], hi_ref[...], NT)
    b = dotf(lj_ref[col, 0:64, :], lo_ref[...], NT)
    yi_ref[row] += md * (a[:64] + a[64:] + b)
    a = dotf(li_ref[row, :, 0:BLOCK], hi_ref[:, 0:BLOCK], NN) + dotf(li_ref[row, :, BLOCK:], hi_ref[:, BLOCK:], NN)
    b = dotf(li_ref[row, 0:64, 0:BLOCK], lo_ref[:, 0:BLOCK], NN) + dotf(li_ref[row, 0:64, BLOCK:], lo_ref[:, BLOCK:], NN)
    yj_ref[col] += mm * (a[:64] + a[64:] + b)

def fill_vectors(b_ref, n, l_ref):
    @pl.loop(0, n)
    def _(k):
        for h in range(2):
            cs = slice(h*BLOCK, (h+1)*BLOCK)
            x = b_ref[k, 0:64, cs] * (b_ref[k, 67:68, cs] * GAIN)
            hi, lo = split(x)
            l_ref[2*k+h, 0:64, 0:BLOCK] = hi
            l_ref[2*k+h, 64:128, 0:BLOCK] = lo
            l_ref[2*k+h, 0:32, BLOCK:] = -hi[32:]
            l_ref[2*k+h, 32:64, BLOCK:] = hi[:32]
            l_ref[2*k+h, 64:96, BLOCK:] = -lo[32:]
            l_ref[2*k+h, 96:128, BLOCK:] = lo[:32]

def compute_kernel(bi_ref, bj_ref, yi_ref, yj_ref,
                   li, lj, p, q, mv, ms, work, hi0, lo0, hi1, lo1, sem):
    ring, zpos, core = place()
    cols = bi_ref[:, 68, 0:128]
    count = bi_ref[:, 69, 0:1]
    lane = lax.broadcasted_iota(jnp.int32, (8, 128), 1)
    cols = jnp.where(lane.astype(jnp.float32) < count, cols, -2.0)
    lane1 = lax.broadcasted_iota(jnp.int32, (8, 128), 1)
    want = (ring + lane1 // 4) * 32 + zpos * 4 + lane1 % 4
    want = jnp.where(lane1 < 12, want, -1).astype(jnp.float32)
    for i in range(2):
        m = jnp.zeros((8, 128), jnp.int32)
        for s in range(i, 96, 2):
            m += jnp.where(jnp.broadcast_to(cols[:, s:s+1], (8, 128)) == want, 1, 0)
        mv[i*8:(i+1)*8, :] = m
    cp = pltpu.make_async_copy(mv, ms, sem)
    cp.start()
    yi_ref[...] = jnp.zeros_like(yi_ref)
    yj_ref[...] = jnp.zeros_like(yj_ref)
    fill_vectors(bi_ref, 8, li)
    fill_vectors(bj_ref, 6, lj)
    @pl.loop(0, 8)
    def _(k):
        t = (bi_ref[k, 64:72, :] * TURN).T
        for h in range(2):
            for d in range(3):
                p[2*k+h, d] = jnp.broadcast_to(t[h*BLOCK:(h+1)*BLOCK, d:d+1], (BLOCK, 128))
    @pl.loop(0, 6)
    def _(k):
        for h in range(2):
            q[2*k+h] = bj_ref[k, 64:72, h*BLOCK:(h+1)*BLOCK] * TURN
    cp.wait()
    def scan_row(rr, n):
        i = rr // 8; zi = rr % 8
        for j in range(12):
            m = ms[rr, j]
            same = jnp.logical_and(zi == zpos, core * 2 + i == j) if j < 4 else False
            work[n] = ((zi*2 + i) * 16 + j) * 256 + m * 2 + (jnp.where(same, 1, 0) if j < 4 else 0)
            n = n + jnp.where(m > 0, 1, 0)
        return n
    n = lax.fori_loop(0, 16, scan_row, jnp.int32(0))
    for e in range(3):
        work[n + e] = 0
    def unpack(t):
        w = work[t]
        row = w // 4096
        col = (w // 256) % 16
        m = (w // 2) % 128
        md = m.astype(jnp.float32)
        mm = jnp.where(w % 2 == 1, 0, m).astype(jnp.float32)
        return row, col, md, mm
    row, col, _, _ = unpack(0)
    build_tile(row, col, p, q, hi0, lo0)
    @pl.loop(0, (n + 1) // 2)
    def _(k):
        r0, c0, d0, m0 = unpack(2*k)
        r1, c1, d1, m1 = unpack(2*k+1)
        r2, c2, _, _ = unpack(2*k+2)
        build_tile(r1, c1, p, q, hi1, lo1)
        apply_tile(r0, c0, d0, m0, li, lj, hi0, lo0, yi_ref, yj_ref)
        build_tile(r2, c2, p, q, hi0, lo0)
        apply_tile(r1, c1, d1, m1, li, lj, hi1, lo1, yi_ref, yj_ref)

VM = pl.BlockSpec(memory_space=pltpu.VMEM)
RINGS = 16
RING_LEN = 8
RULES = 4
SLOTS = 96


def place():
    me = lax.axis_index("band") * 32 + lax.axis_index("dev")
    return me // 16, (me // 2) % 8, me % 2


def device(ring, z, core):
    k = (ring % RINGS) * 16 + (z % RING_LEN) * 2 + core
    return (k // 32, k % 32)


def remote(src, dst, ssem, rsem, target):
    return pltpu.make_async_remote_copy(
        src_ref=src, dst_ref=dst, send_sem=ssem, recv_sem=rsem,
        device_id=target, device_id_type=pl.DeviceIdType.MESH,
    )


def greet(ring, z, core):
    barrier = pltpu.get_barrier_semaphore()
    peers = [device(ring, z + 1, core), device(ring, z - 1, core), device(ring, z, 1 - core)]
    for d in (1, -1, 2, -2):
        for c in range(2):
            peers.append(device(ring + d, z, c))
    for peer in peers:
        pl.semaphore_signal(barrier, inc=1, device_id=peer, device_id_type=pl.DeviceIdType.MESH)
    pl.semaphore_wait(barrier, len(peers))


CUTS = ((0, 40), (40, 72))
HOPS = 4


def gather_kernel(b_ref, bi_ref, bj_ref, ring_send, ring_recv, side_send, side_recv, own_sem):
    ring, z, core = place()
    greet(ring, z, core)
    started = []

    def hop(way, h, ch):
        step = 1 - 2 * way
        owner = (z - step * h) % RING_LEN
        lo, hi = CUTS[ch]
        rows = pl.ds(lo, hi - lo)
        src = b_ref.at[rows] if h == 0 else bi_ref.at[owner, rows]
        cp = remote(src, bi_ref.at[owner, rows], ring_send.at[way, h, ch], ring_recv.at[way, h, ch],
                    device(ring, z + step, core))
        return cp

    def used(way, h, ch):
        return h < HOPS - 1 or ch == way

    for ch in range(2):
        for way in range(2):
            cp = hop(way, 0, ch)
            cp.start()
            started.append(cp)
    sides = [(1, 0), (1, 1), (2, 0), (2, 1)]
    for n, (d, c) in enumerate(sides):
        cp = remote(b_ref, bj_ref.at[d * 2 + core], side_send.at[n], side_recv.at[d * 2 + core],
                    device(ring - d, z, c))
        cp.start()
        started.append(cp)
    cp = remote(b_ref, bj_ref.at[core], side_send.at[4], side_recv.at[core], device(ring, z, 1 - core))
    cp.start()
    started.append(cp)
    mine = [pltpu.make_async_copy(b_ref, bi_ref.at[z], own_sem.at[0]),
            pltpu.make_async_copy(b_ref, bj_ref.at[core], own_sem.at[1])]
    for cp in mine:
        cp.start()
    for h in range(1, HOPS):
        for ch in range(2):
            for way in range(2):
                hop(way, h - 1, ch).wait_recv()
                if used(way, h, ch):
                    cp = hop(way, h, ch)
                    cp.start()
                    started.append(cp)
    for way in range(2):
        hop(way, HOPS - 1, way).wait_recv()
    for d in (1, 2):
        for c in range(2):
            remote(b_ref, bj_ref.at[d * 2 + c], side_send.at[0], side_recv.at[d * 2 + c],
                   device(ring, z, 1 - core)).wait_recv()
    remote(b_ref, bj_ref.at[1 - core], side_send.at[4], side_recv.at[1 - core],
           device(ring, z, 1 - core)).wait_recv()
    for cp in started:
        cp.wait_send()
    for cp in mine:
        cp.wait()


def gather(b):
    f = jnp.float32
    dma = pltpu.SemaphoreType.DMA
    return pl.pallas_call(
        gather_kernel,
        out_shape=(jax.ShapeDtypeStruct((8, 72, 512), f), jax.ShapeDtypeStruct((6, 72, 512), f)),
        in_specs=[VM], out_specs=(VM, VM),
        scratch_shapes=[dma((2, HOPS, 2)), dma((2, HOPS, 2)), dma((5,)), dma((6,)), dma((2,))],
        compiler_params=pltpu.CompilerParams(collective_id=0, has_side_effects=True, vmem_limit_bytes=16 << 20),
    )(b)


def compute(bi, bj):
    f = jnp.float32
    b = jnp.bfloat16
    return pl.pallas_call(
        compute_kernel,
        out_shape=(jax.ShapeDtypeStruct((16, 64, 256), f), jax.ShapeDtypeStruct((12, 64, 256), f)),
        in_specs=[VM] * 2, out_specs=(VM, VM),
        scratch_shapes=[pltpu.VMEM((16, 128, 512), b), pltpu.VMEM((12, 128, 512), b),
                        pltpu.VMEM((16, 3, 256, 128), f), pltpu.VMEM((12, 8, 256), f),
                        pltpu.VMEM((16, 128), jnp.int32), pltpu.SMEM((16, 128), jnp.int32),
                        pltpu.SMEM((256,), jnp.int32),
                        pltpu.VMEM((256, 512), b), pltpu.VMEM((256, 512), b),
                        pltpu.VMEM((256, 512), b), pltpu.VMEM((256, 512), b),
                        pltpu.SemaphoreType.DMA],
        compiler_params=pltpu.CompilerParams(vmem_limit_bytes=48 << 20),
    )(bi, bj)


def reduce_kernel(yi_ref, yj_ref, w_ref, out_ref, flow, side, ring_send, ring_recv, side_send, side_recv):
    ring, z, core = place()
    greet(ring, z, core)
    started = []

    def part(ref, first, ch):
        return ref.at[pl.ds(first, 2), pl.ds(32 * ch, 32)]

    def hop(way, h, ch, src):
        step = 1 - 2 * way
        cp = remote(src, part(flow.at[way, h], 0, ch), ring_send.at[way, h, ch], ring_recv.at[way, h, ch],
                    device(ring, z + step, core))
        return cp

    def target(way, h):
        return (z + (1 - 2 * way) * (HOPS - h)) % RING_LEN

    def launch(cp):
        cp.start()
        started.append(cp)

    for way in range(2):
        launch(hop(way, 0, way, part(yi_ref, 2 * target(way, 0), way)))
    for way in range(2):
        launch(hop(way, 1, 1 - way, part(yi_ref, 2 * target(way, 1), 1 - way)))
    n = 0
    for d in (1, 2):
        for c in range(2):
            launch(remote(yj_ref.at[pl.ds((d * 2 + c) * 2, 2)], side.at[(d - 1) * 2 + core], side_send.at[n],
                          side_recv.at[(d - 1) * 2 + core], device(ring + d, z, c)))
            n += 1
    launch(remote(yj_ref.at[pl.ds((1 - core) * 2, 2)], side.at[4], side_send.at[4], side_recv.at[4],
                  device(ring, z, 1 - core)))
    for h in range(1, HOPS):
        for k in range(2):
            for way in range(2):
                ch = way if k == 0 else 1 - way
                if k == 1 and h == 1:
                    continue
                here = part(flow.at[way, h - 1], 0, ch)
                hop(way, h - 1, ch, here).wait_recv()
                rows = slice(32 * ch, 32 * ch + 32)
                flow[way, h - 1, :, rows, :] += yi_ref[pl.ds(2 * target(way, h), 2), rows, :]
                launch(hop(way, h, ch, here))
    for way in range(2):
        for ch in range(2):
            hop(way, HOPS - 1, ch, part(flow.at[way, 0], 0, ch)).wait_recv()
    for s in range(5):
        remote(side.at[s], side.at[s], side_send.at[s], side_recv.at[s], device(ring, z, 1 - core)).wait_recv()
    for h in range(2):
        total = yi_ref[2 * z + h] + yj_ref[2 * core + h]
        total += side[0, h] + side[1, h] + (side[2, h] + side[3, h]) + side[4, h]
        total += flow[0, HOPS - 1, h] + flow[1, HOPS - 1, h]
        out_ref[:, h * BLOCK:(h + 1) * BLOCK] = total * w_ref[3:4, h * BLOCK:(h + 1) * BLOCK]
    for cp in started:
        cp.wait_send()


def reduce(yi, yj, aux):
    f = jnp.float32
    dma = pltpu.SemaphoreType.DMA
    return pl.pallas_call(
        reduce_kernel,
        out_shape=jax.ShapeDtypeStruct((64, 512), f),
        in_specs=[VM] * 3, out_specs=VM,
        scratch_shapes=[pltpu.VMEM((2, HOPS, 2, 64, 256), f), pltpu.VMEM((5, 2, 64, 256), f),
                        dma((2, HOPS, 2)), dma((2, HOPS, 2)), dma((5,)), dma((5,))],
        compiler_params=pltpu.CompilerParams(collective_id=1, has_side_effects=True, vmem_limit_bytes=16 << 20),
    )(yi, yj, aux)


def body(drive, coords, rule_index, rule_weight, pair_cols, pair_count):
    weights = jnp.zeros((512,), jnp.float32)
    for r in range(RULES):
        weights = jnp.where(rule_index == r, rule_weight[r], weights)
    cols = jnp.pad(pair_cols.astype(jnp.float32), (0, 512 - SLOTS))
    count = jnp.broadcast_to(pair_count.astype(jnp.float32), (512,))
    aux = jnp.concatenate([coords, jnp.stack([weights, cols, count, count, count])], axis=0)
    b = jnp.concatenate([drive.reshape(64, 512), aux], axis=0)
    bi, bj = gather(b)
    yi, yj = compute(bi, bj)
    return reduce(yi, yj, aux).reshape(2, 32, 512)


def solution(mesh):
    both = ("band", "dev")
    in_specs = (P(None, None, both), P(None, both), P(both), P(), P(both), P(both))
    return jax.shard_map(body, mesh=mesh, in_specs=in_specs, out_specs=P(None, None, both), check_vma=False)
```

time: 1470 us -> 84 us (0.06)
  the two profiles are of different devices: /device:TPU:1 before, /device:TPU:10 now
where the time goes in v1:
time: 84 us; the launch traced here: 82.4 us
  Pallas kernels  74.2 us (88%)
  other arithmetic  3.77 us (4%)
  local copies, waits for them, and re-layouts  3.75 us (4%)
    pallas_call x1, Pallas kernels, reduce(): pl.pallas_call(reduce_kernel, out_shape=jax.ShapeDtypeStruct((64, 512), f...  31.2 us
    pallas_call x1, Pallas kernels, gather(): pl.pallas_call(gather_kernel, out_shape=(jax.ShapeDtypeStruct((8, 72, 512...  24.4 us
    pallas_call x1, Pallas kernels, compute(): pl.pallas_call(compute_kernel, out_shape=(jax.ShapeDtypeStruct((16, 64, 2...  18.5 us
    select_n x1, other arithmetic, body(): weights = jnp.where(rule_index == r, rule_weight[r], weights)  3.11 us

profile of v1, /device:TPU:10, one launch (start us, length us, event | category | flops | bytes accessed | tf_op | source)
XLA Modules:
  0.0 82.4 jit_solution(12034325804258442602)
XLA Ops:
  0.0 1.4 %fusion = (f32[1]{0:T(128)}, f32[1]{0:T(128)}, f32[1]{0:T(128)}, f32[1]{0:T(128)}) fusion(f32[4]{0:T(128)} %param.9), kind=kLoop, calls=%fused_computation.1 | loop fusion | bytes 32 | tf_op jit(solution)/shard_map/slice | solution.py:349
  1.4 3.1 %select_select_fusion = f32[512]{0:T(512)S(1)} fusion(s32[512]{0:T(512)} %param.8, f32[]{:T(128)} %bitcast.4, f32[]{:T(128)} %bitcast.3, f32[]{:T(128)} %bitcast.2, f32[]{:T(128)} %bitcast.1), kind=kLoop, calls=%fused_computation | loop fusion | flops 4096 | bytes 4112 | tf_op jit(solution)/shard_map/jit(_where)/select_n | solution.py:349
  5.2 0.7 convert_element_type.10
  5.9 1.6 %concatenate.7.b_ref = f32[72,512]{1,0:T(8,128)S(1)} concatenate(f32[64,512]{1,0:T(8,128)} %bitcast.10, f32[3,512]{1,0:T(4,128)} %param.7, f32[1,512]{1,0:T(1,128)S(1)} %bitcast.11, f32[1,512]{1,0:T(1,128)S(1)} %bitcast.13, f32[1,512]{1,0:T(1,128)S(1)} %stack_broadcast_in_dim.2, f32[1,512]{1,0:T(1,128)S(1)} %stack_broadcast_in_dim.2, f32[1,512]{1,0:T(1,128)S(1)} %stack_broadcast_in_dim.2), dimensions={0} | concatenate | bytes 294912 | tf_op jit(solution)/shard_map/concatenate | solution.py:353
  7.5 0.0 copy-start
  7.5 24.4 %shard_map.64 = (f32[8,72,512]{2,1,0:T(8,128)S(1)}, f32[6,72,512]{2,1,0:T(8,128)S(1)}) custom-call(f32[72,512]{1,0:T(8,128)S(1)} %concatenate.7.b_ref), custom_call_target="tpu_custom_call" | custom-call | tf_op jit(solution)/shard_map/pallas_call | solution.py:248
  31.9 18.5 %shard_map.65 = (f32[16,64,256]{2,1,0:T(8,128)S(1)}, f32[12,64,256]{2,1,0:T(8,128)S(1)}) custom-call(f32[8,72,512]{2,1,0:T(8,128)S(1)} %get-tuple-element.9.bi_ref, f32[6,72,512]{2,1,0:T(8,128)S(1)} %get-tuple-element.10.bj_ref), custom_call_target="tpu_custom_call" | custom-call | tf_op jit(solution)/shard_map/pallas_call | solution.py:260
  50.4 0.0 copy-done
  50.5 31.2 %shard_map.66 = f32[64,512]{1,0:T(8,128)S(1)} custom-call(f32[16,64,256]{2,1,0:T(8,128)S(1)} %get-tuple-element.11.yi_ref, f32[12,64,256]{2,1,0:T(8,128)S(1)} %get-tuple-element.12.yj_ref, f32[8,512]{1,0:T(8,128)S(1)} %concatenate.8.w_ref), custom_call_target="tpu_custom_call" | custom-call | tf_op jit(solution)/shard_map/pallas_call | solution.py:336
  81.7 0.7 copy.9
  (3 shorter events, 0.0 us)
Async XLA Ops:
  7.5 43.0 %copy-start = (f32[3,512]{1,0:T(4,128)S(1)}, f32[3,512]{1,0:T(4,128)}, u32[]{:S(2)}) copy-start(f32[3,512]{1,0:T(4,128)} %param.7) | copy-start | bytes 18436

commit v2 on v0

v2 whole, which is shorter than its diff:
```python
import math

import jax
import jax.numpy as jnp
from jax import lax
from jax.experimental import pallas as pl
from jax.experimental.pallas import tpu as pltpu
from jax.sharding import PartitionSpec as P

BLOCK = 256
RULES = 4
SLOTS = 96
RINGS = 16
RING_LEN = 8
HOPS = 4
ROWS = 32
PACK = 72
WAVES = 25.0 / (2.0 * math.pi)
GAIN = 25.0 / (8.0 * math.pi**2)
SMOOTH = (0.05 * WAVES) ** 2
SINE = (2.6417539924711972, -1.0863767471480779, 0.1340056362838771, -0.007739908243745813)
FULL = 2.0 * math.sqrt(2.0)
HALF = math.sqrt(2.0)

VM = pl.BlockSpec(memory_space=pltpu.VMEM)
SM = pl.BlockSpec(memory_space=pltpu.SMEM)
MESH = pl.DeviceIdType.MESH
NT = (((1,), (1,)), ((), ()))
NN = (((1,), (0,)), ((), ()))


def place():
    me = lax.axis_index("band") * 32 + lax.axis_index("dev")
    return me // 16, (me // 2) % 8, me % 2


def device(ring, z, core):
    k = (ring % RINGS) * 16 + (z % RING_LEN) * 2 + core
    return (k // 32, k % 32)


def remote(src, dst, ssem, rsem, target):
    return pltpu.make_async_remote_copy(
        src_ref=src, dst_ref=dst, send_sem=ssem, recv_sem=rsem, device_id=target, device_id_type=MESH
    )


def partners(ring, z, core):
    peers = [device(ring, z + 1, core), device(ring, z - 1, core), device(ring, z, 1 - core)]
    for d in (1, -1, 2, -2):
        for c in range(2):
            peers.append(device(ring + d, z, c))
    return peers


def split(v):
    hi = v.astype(jnp.bfloat16)
    return hi, (v - hi.astype(jnp.float32)).astype(jnp.bfloat16)


def fill_vectors(src, slot, l_ref):
    for h in range(2):
        hi, lo = split(src[0:64, h * BLOCK:(h + 1) * BLOCK])
        k = 2 * slot + h
        l_ref[k, 0:64, 0:BLOCK] = hi
        l_ref[k, 64:128, 0:BLOCK] = lo
        l_ref[k, 0:32, BLOCK:] = -hi[32:]
        l_ref[k, 32:64, BLOCK:] = hi[:32]
        l_ref[k, 64:96, BLOCK:] = -lo[32:]
        l_ref[k, 96:128, BLOCK:] = lo[:32]


CUTS = ((0, 40), (40, PACK))


def gather_kernel(x_ref, c_ref, rule_ref, rw_ref, cols_ref, count_ref,
                  li_ref, lj_ref, p_ref, q_ref, table_ref, w_ref,
                  b_ref, bi_ref, bj_ref, ring_send, ring_recv, side_send, side_recv):
    ring, z, core = place()
    barrier = pltpu.get_barrier_semaphore()
    peers = partners(ring, z, core)
    for peer in peers:
        pl.semaphore_signal(barrier, inc=1, device_id=peer, device_id_type=MESH)

    rule = rule_ref[...]
    w = jnp.zeros((1, 512), jnp.float32)
    for r in range(RULES):
        w = jnp.where(rule == r, rw_ref[r], w)
    w_ref[...] = jnp.broadcast_to(w, (8, 512))
    b_ref[0:64, :] = x_ref[...] * (w * GAIN)
    b_ref[64:67, :] = c_ref[...] * WAVES
    b_ref[67:72, :] = jnp.full((5, 512), -2.0, jnp.float32)
    slot = lax.broadcasted_iota(jnp.int32, (1, SLOTS), 1)
    b_ref[67:68, 0:SLOTS] = jnp.where(slot < count_ref[0], cols_ref[...], -2).astype(jnp.float32)
    table_ref[...] = jnp.zeros_like(table_ref)

    pl.semaphore_wait(barrier, len(peers))
    started = []

    def launch(cp):
        cp.start()
        started.append(cp)

    def owner_of(way, h):
        return (z - (1 - 2 * way) * h) % RING_LEN

    def hop(way, h, ch):
        owner = owner_of(way, h)
        rows = pl.ds(CUTS[ch][0], CUTS[ch][1] - CUTS[ch][0])
        src = b_ref.at[rows] if h == 0 else bi_ref.at[owner, rows]
        return remote(src, bi_ref.at[owner, rows], ring_send.at[way, h, ch], ring_recv.at[way, h, ch],
                      device(ring, z + 1 - 2 * way, core))

    for ch in range(2):
        for way in range(2):
            launch(hop(way, 0, ch))
    for n, (d, c) in enumerate(((1, 0), (1, 1), (2, 0), (2, 1))):
        launch(remote(b_ref, bj_ref.at[d * 2 + core], side_send.at[n],
                      side_recv.at[d * 2 + core], device(ring - d, z, c)))
    launch(remote(b_ref, bj_ref.at[core], side_send.at[4], side_recv.at[core],
                  device(ring, z, 1 - core)))

    lane = lax.broadcasted_iota(jnp.int32, (16, 128), 1)
    col = lax.broadcasted_iota(jnp.int32, (16, 128), 0)
    want = jnp.where(col < 12, (ring + col // 4) * 32 + z * 4 + col % 4, -1).astype(jnp.float32)

    def expand_i(src, k):
        fill_vectors(src, k, li_ref)
        t = src[64:72, :].T
        for h in range(2):
            for d in range(3):
                p_ref[2 * k + h, d] = jnp.broadcast_to(t[h * BLOCK:(h + 1) * BLOCK, d:d + 1], (BLOCK, 128))
        hit = jnp.where(jnp.broadcast_to(src[67:68, 0:128], (16, 128)) == want, 1.0, 0.0)
        for i in range(2):
            m = jnp.sum(jnp.where(lane % 2 == i, hit, 0.0), axis=1, keepdims=True)
            table_ref[...] += jnp.where(lane == 2 * k + i, m, 0.0).astype(jnp.int32)

    def expand_j(src, k):
        fill_vectors(src, k, lj_ref)
        for h in range(2):
            q_ref[2 * k + h] = src[64:72, h * BLOCK:(h + 1) * BLOCK]

    expand_i(b_ref, z)
    expand_j(b_ref, core)
    for h in range(1, HOPS):
        for ch in range(2):
            for way in range(2):
                hop(way, h - 1, ch).wait_recv()
                if h < HOPS - 1 or ch == way:
                    launch(hop(way, h, ch))
        for way in range(2):
            k = owner_of(way, h)
            expand_i(bi_ref.at[k], k)
        js = ((1 - core, 4),) if h == 1 else ((4, 0), (5, 0)) if h == 2 else ((2, 0), (3, 0))
        for k, n in js:
            remote(b_ref, bj_ref.at[k], side_send.at[n], side_recv.at[k],
                   device(ring, z, 1 - core)).wait_recv()
            expand_j(bj_ref.at[k], k)
    for way in range(2):
        hop(way, HOPS - 1, way).wait_recv()
    k = (z + HOPS) % RING_LEN
    expand_i(bi_ref.at[k], k)
    for cp in started:
        cp.wait_send()


def gather(x, coords, rule, rw, cols, count):
    f = jnp.float32
    b = jnp.bfloat16
    dma = pltpu.SemaphoreType.DMA
    s = jax.ShapeDtypeStruct
    return pl.pallas_call(
        gather_kernel,
        out_shape=(s((16, 128, 512), b), s((12, 128, 512), b), s((16, 3, 256, 128), f), s((12, 8, 256), f),
                   s((16, 128), jnp.int32), s((8, 512), f)),
        in_specs=[VM, VM, VM, SM, VM, SM],
        out_specs=(VM,) * 6,
        scratch_shapes=[pltpu.VMEM((PACK, 512), f), pltpu.VMEM((8, PACK, 512), f), pltpu.VMEM((6, PACK, 512), f),
                        dma((2, HOPS, 2)), dma((2, HOPS, 2)), dma((5,)), dma((6,))],
        compiler_params=pltpu.CompilerParams(collective_id=0, has_side_effects=True, vmem_limit_bytes=20 << 20),
    )(x, coords, rule, rw, cols, count)


def build_tile(row, col, p_ref, q_ref, hi_ref, lo_ref):
    qx = q_ref[col, 0:1, :]
    qy = q_ref[col, 1:2, :]
    qz = q_ref[col, 2:3, :]
    for r in range(0, BLOCK, ROWS):
        px = p_ref[row, 0, r:r + ROWS, :]
        py = p_ref[row, 1, r:r + ROWS, :]
        pz = p_ref[row, 2, r:r + ROWS, :]
        dx = jnp.concatenate([px, px], axis=1) - qx
        dy = jnp.concatenate([py, py], axis=1) - qy
        dz = jnp.concatenate([pz, pz], axis=1) - qz
        square = dx * dx + (dy * dy + (dz * dz + SMOOTH))
        inv = lax.rsqrt(square)
        turns = square * inv
        f = turns - jnp.round(turns)
        f2 = f * f
        poly = SINE[-1]
        for k in SINE[-2::-1]:
            poly = poly * f2 + k
        s = f * poly
        ss = s * s
        rest = FULL - ss
        sh = s * (rest * lax.rsqrt(rest))
        ch = HALF - ss
        t = inv * sh
        rh, rl = split(inv - t * sh)
        ih, il = split(t * ch)
        hi_ref[r:r + ROWS, 0:BLOCK] = rh
        hi_ref[r:r + ROWS, BLOCK:] = ih
        lo_ref[r:r + ROWS, 0:BLOCK] = rl
        lo_ref[r:r + ROWS, BLOCK:] = il


def dotf(a, b, dims):
    return lax.dot_general(a, b, dims, preferred_element_type=jnp.float32)


def apply_tile(row, col, md, mm, li_ref, lj_ref, hi_ref, lo_ref, yi_ref, yj_ref):
    a = dotf(lj_ref[col], hi_ref[...], NT)
    b = dotf(lj_ref[col, 0:64, :], lo_ref[...], NT)
    yi_ref[row] += md * (a[:64] + a[64:] + b)
    a = dotf(li_ref[row, :, 0:BLOCK], hi_ref[:, 0:BLOCK], NN) + dotf(li_ref[row, :, BLOCK:], hi_ref[:, BLOCK:], NN)
    b = dotf(li_ref[row, 0:64, 0:BLOCK], lo_ref[:, 0:BLOCK], NN) + dotf(
        li_ref[row, 0:64, BLOCK:], lo_ref[:, BLOCK:], NN)
    yj_ref[col] += mm * (a[:64] + a[64:] + b)


def compute_kernel(li, lj, p, q, table, yi_ref, yj_ref, counts, work, hi0, lo0, hi1, lo1, sem):
    _, z, core = place()
    cp = pltpu.make_async_copy(table, counts, sem)
    cp.start()
    yi_ref[...] = jnp.zeros_like(yi_ref)
    yj_ref[...] = jnp.zeros_like(yj_ref)
    cp.wait()

    def scan_row(row, n):
        for j in range(12):
            m = counts[j, row]
            code = row * 4096 + j * 256 + m * 2
            work[n] = code
            n = n + jnp.where(m > 0, 1, 0)
        return n

    n = lax.fori_loop(0, 16, scan_row, jnp.int32(0))
    for e in range(3):
        work[n + e] = 0

    def unpack(t):
        w = work[t]
        row = lax.shift_right_logical(w, 12)
        col = lax.shift_right_logical(w, 8) & 15
        m = lax.shift_right_logical(w, 1) & 127
        same = jnp.logical_and(lax.shift_right_logical(row, 1) == z, col == core * 2 + (row & 1))
        return row, col, m.astype(jnp.float32), jnp.where(same, 0, m).astype(jnp.float32)

    row, col, _, _ = unpack(0)
    build_tile(row, col, p, q, hi0, lo0)

    @pl.loop(0, (n + 1) // 2)
    def _(k):
        r0, c0, d0, m0 = unpack(2 * k)
        r1, c1, d1, m1 = unpack(2 * k + 1)
        r2, c2, _, _ = unpack(2 * k + 2)
        build_tile(r1, c1, p, q, hi1, lo1)
        apply_tile(r0, c0, d0, m0, li, lj, hi0, lo0, yi_ref, yj_ref)
        build_tile(r2, c2, p, q, hi0, lo0)
        apply_tile(r1, c1, d1, m1, li, lj, hi1, lo1, yi_ref, yj_ref)


def compute(li, lj, p, q, table):
    f = jnp.float32
    b = jnp.bfloat16
    return pl.pallas_call(
        compute_kernel,
        out_shape=(jax.ShapeDtypeStruct((16, 64, 256), f), jax.ShapeDtypeStruct((12, 64, 256), f)),
        in_specs=[VM] * 5, out_specs=(VM, VM),
        scratch_shapes=[pltpu.SMEM((16, 128), jnp.int32), pltpu.SMEM((256,), jnp.int32),
                        pltpu.VMEM((256, 512), b), pltpu.VMEM((256, 512), b),
                        pltpu.VMEM((256, 512), b), pltpu.VMEM((256, 512), b),
                        pltpu.SemaphoreType.DMA],
        compiler_params=pltpu.CompilerParams(vmem_limit_bytes=24 << 20),
    )(li, lj, p, q, table)


def reduce_kernel(yi_ref, yj_ref, w_ref, out_ref, flow, side, ring_send, ring_recv, side_send, side_recv):
    ring, z, core = place()
    barrier = pltpu.get_barrier_semaphore()
    peers = partners(ring, z, core)
    for peer in peers:
        pl.semaphore_signal(barrier, inc=1, device_id=peer, device_id_type=MESH)
    pl.semaphore_wait(barrier, len(peers))
    started = []

    def part(ref, first, ch):
        return ref.at[pl.ds(first, 2), pl.ds(32 * ch, 32)]

    def hop(way, h, ch, src):
        return remote(src, part(flow.at[way, h], 0, ch), ring_send.at[way, h, ch], ring_recv.at[way, h, ch],
                      device(ring, z + 1 - 2 * way, core))

    def target(way, h):
        return (z + (1 - 2 * way) * (HOPS - h)) % RING_LEN

    def launch(cp):
        cp.start()
        started.append(cp)

    for way in range(2):
        launch(hop(way, 0, way, part(yi_ref, 2 * target(way, 0), way)))
    for way in range(2):
        launch(hop(way, 1, 1 - way, part(yi_ref, 2 * target(way, 1), 1 - way)))
    n = 0
    for d in (1, 2):
        for c in range(2):
            launch(remote(yj_ref.at[pl.ds((d * 2 + c) * 2, 2)], side.at[(d - 1) * 2 + core], side_send.at[n],
                          side_recv.at[(d - 1) * 2 + core], device(ring + d, z, c)))
            n += 1
    launch(remote(yj_ref.at[pl.ds((1 - core) * 2, 2)], side.at[4], side_send.at[4], side_recv.at[4],
                  device(ring, z, 1 - core)))
    for h in range(1, HOPS):
        for k in range(2):
            for way in range(2):
                ch = way if k == 0 else 1 - way
                if k == 1 and h == 1:
                    continue
                here = part(flow.at[way, h - 1], 0, ch)
                hop(way, h - 1, ch, here).wait_recv()
                rows = slice(32 * ch, 32 * ch + 32)
                flow[way, h - 1, :, rows, :] += yi_ref[pl.ds(2 * target(way, h), 2), rows, :]
                launch(hop(way, h, ch, here))
    for way in range(2):
        for ch in range(2):
            hop(way, HOPS - 1, ch, part(flow.at[way, 0], 0, ch)).wait_recv()
    for s in range(5):
        remote(side.at[s], side.at[s], side_send.at[s], side_recv.at[s], device(ring, z, 1 - core)).wait_recv()
    for h in range(2):
        total = yi_ref[2 * z + h] + yj_ref[2 * core + h]
        total += side[0, h] + side[1, h] + (side[2, h] + side[3, h]) + side[4, h]
        total += flow[0, HOPS - 1, h] + flow[1, HOPS - 1, h]
        out_ref[:, h * BLOCK:(h + 1) * BLOCK] = total * w_ref[0:1, h * BLOCK:(h + 1) * BLOCK]
    for cp in started:
        cp.wait_send()


def reduce(yi, yj, w):
    f = jnp.float32
    dma = pltpu.SemaphoreType.DMA
    return pl.pallas_call(
        reduce_kernel,
        out_shape=jax.ShapeDtypeStruct((64, 512), f),
        in_specs=[VM] * 3, out_specs=VM,
        scratch_shapes=[pltpu.VMEM((2, HOPS, 2, 64, 256), f), pltpu.VMEM((5, 2, 64, 256), f),
                        dma((2, HOPS, 2)), dma((2, HOPS, 2)), dma((5,)), dma((5,))],
        compiler_params=pltpu.CompilerParams(collective_id=1, has_side_effects=True, vmem_limit_bytes=16 << 20),
    )(yi, yj, w)


def body(drive, coords, rule_index, rule_weight, pair_cols, pair_count):
    li, lj, p, q, table, w = gather(drive.reshape(64, 512), coords, rule_index.reshape(1, 512), rule_weight,
                                    pair_cols.reshape(1, SLOTS), pair_count)
    yi, yj = compute(li, lj, p, q, table)
    return reduce(yi, yj, w).reshape(2, 32, 512)


def solution(mesh):
    both = ("band", "dev")
    in_specs = (P(None, None, both), P(None, both), P(both), P(), P(both), P(both))
    return jax.shard_map(body, mesh=mesh, in_specs=in_specs, out_specs=P(None, None, both), check_vma=False)
```

time: 1470 us -> 78.6 us (0.05); the launches traced: 1450 us -> 78 us
  waiting for transfers between devices: 1020 us -> 0 us
  matrix products: 171 us -> 0 us
  other arithmetic: 115 us -> 0 us
  Pallas kernels: 0 us -> 73 us
  loops' own time: 41.6 us -> 0 us
  blocking collectives: 38.7 us -> 0 us
  local copies, waits for them, and re-layouts: 41.9 us -> 4.24 us
    reduce_scatter x1 -> x0, waiting for transfers between devices: 823 us -> none  [body(): lax.psum_scatter(own_part + carried, 'dev', scatter_dimension=2, tiled=True)]
    dot_general x16 -> x0, matrix products: 171 us -> none  [the longest x8 86 us: batch_apply(): jnp.einsum(form, vectors, imag_part, precision=highest, preferred_element...]
    ppermute x3 -> x0, waiting for transfers between devices: 101 us -> none  [from_behind(): lax.ppermute(value, axis, [(source, source + steps) for source in range(i...]
    dynamic_update_slice x64 -> x0, other arithmetic: 94.8 us -> none  [add_block(): lax.dynamic_update_slice_in_dim(accumulated, previous + update_block, blo...]
    all_gather x1 -> x0, waiting for transfers between devices: 93.7 us -> none  [body(): lax.all_gather(drive, 'dev', axis=2, tiled=True)]
    pallas_call x0 -> x3, Pallas kernels: none -> 73 us  [the longest x1 28.6 us: reduce(): pl.pallas_call(reduce_kernel, out_shape=jax.ShapeDtypeStruct((64, 512), f...]
    another operation x1 -> x0, loops' own time: 41.6 us -> none  [body(): accumulated = lax.fori_loop(0, turns, one_turn, accumulated)]
    all_gather x1 -> x0, blocking collectives: 38.7 us -> none  [body(): lax.all_gather(geometry, 'dev', axis=1, tiled=True)]
  transfers between devices with their start and end apart: 5 -> 0, of which waited for: 4 -> 0; matrix products, arithmetic and copies ran while one was open for 0% -> 0% of each run, Pallas kernels for 0% -> 0%
where the time goes in v2:
time: 78.6 us; the launch traced here: 78 us
  Pallas kernels  73 us (93%)
  local copies, waits for them, and re-layouts  4.24 us (5%)
    pallas_call x1, Pallas kernels, reduce(): pl.pallas_call(reduce_kernel, out_shape=jax.ShapeDtypeStruct((64, 512), f...  28.6 us
    pallas_call x1, Pallas kernels, gather(): pl.pallas_call(gather_kernel, out_shape=(s((16, 128, 512), b), s((12, 128...  25.9 us
    pallas_call x1, Pallas kernels, compute(): pl.pallas_call(compute_kernel, out_shape=(jax.ShapeDtypeStruct((16, 64, 2...  18.5 us
    unnamed x11, local copies, waits for them, and re-layouts  4.24 us

profile of v2, /device:TPU:1, one launch (start us, length us, event | category | flops | bytes accessed | tf_op | source)
XLA Modules:
  0.0 78.0 jit_solution(17092196130991158076)
XLA Ops:
  0.7 0.0 copy-start
  0.7 0.9 %copy-done = f32[2,32,512]{2,1,0:T(8,128)S(1)} copy-done((f32[2,32,512]{2,1,0:T(8,128)S(1)}, f32[2,32,512]{2,1,0:T(8,128)}, u32[]{:S(2)}) %copy-start) | copy-done | bytes 131096
  1.6 0.0 copy-start.1
  1.6 0.7 copy-done.1
  2.3 0.0 copy-start.2
  2.3 0.7 copy-done.2
  2.9 0.0 copy-start.3
  2.9 0.7 copy-done.3
  3.6 0.0 copy-start.4
  3.6 0.7 copy-done.4
  4.2 25.9 %shard_map.64 = (bf16[16,128,512]{2,1,0:T(8,128)(2,1)S(1)}, bf16[12,128,512]{2,1,0:T(8,128)(2,1)S(1)}, f32[16,3,256,128]{3,2,1,0:T(8,128)S(1)}, f32[12,8,256]{2,...) custom-call(f32[64,512]{1,0:T(8,128)S(1)} %bitcast.5, f32[3,512]{1,0:T(4,128)S(1)} %copy-done.1, ...), custom_call_target="tpu_custom_call" | custom-call | tf_op jit(solution)/shard_map/pallas_call | solution.py:172
  30.2 18.5 %shard_map.65 = (f32[16,64,256]{2,1,0:T(8,128)S(1)}, f32[12,64,256]{2,1,0:T(8,128)S(1)}) custom-call(bf16[16,128,512]{2,1,0:T(8,128)(2,1)S(1)} %get-tuple-element.13.li, bf16[12,128,512]{2,1,0:T(8,128)(2,1)S(1)} %get-tuple-element.14.lj, f32[16,3,256,128]{3,2,1,0:T(8,128)S(1)} %get-tuple-element.15.p, f32[12,8,256]{2,1,0:T(8,128)S(1)} %get-tuple-element.16.q, ...), custom_call_target="tpu_custom_call" | custom-call | tf_op jit(solution)/shard_map/pallas_call | solution.py:276
  48.7 28.6 %shard_map.66 = f32[64,512]{1,0:T(8,128)S(1)} custom-call(f32[16,64,256]{2,1,0:T(8,128)S(1)} %get-tuple-element.18.yi_ref, f32[12,64,256]{2,1,0:T(8,128)S(1)} %get-tuple-element.19.yj_ref, f32[8,512]{1,0:T(8,128)S(1)} %get-tuple-element.20.w_ref), custom_call_target="tpu_custom_call" | custom-call | tf_op jit(solution)/shard_map/pallas_call | solution.py:351
  77.3 0.7 copy.9
Async XLA Ops:
  0.7 0.9 %copy-start = (f32[2,32,512]{2,1,0:T(8,128)S(1)}, f32[2,32,512]{2,1,0:T(8,128)}, u32[]{:S(2)}) copy-start(f32[2,32,512]{2,1,0:T(8,128)} %param.6) | copy-start | bytes 393220
  1.6 0.7 copy-start.1
  2.3 0.7 copy-start.2
  2.9 0.7 copy-start.3
  3.6 0.7 copy-start.4

commit v3 on v2

--- a/solution.py
+++ b/solution.py
@@ -23,7 +23,7 @@
 HALF = math.sqrt(2.0)
 
 VM = pl.BlockSpec(memory_space=pltpu.VMEM)
-SM = pl.BlockSpec(memory_space=pltpu.SMEM)
+HBM = pl.BlockSpec(memory_space=pltpu.HBM)
 MESH = pl.DeviceIdType.MESH
 NT = (((1,), (1,)), ((), ()))
 NN = (((1,), (0,)), ((), ()))
@@ -70,18 +70,30 @@
         l_ref[k, 96:128, BLOCK:] = lo[:32]
 
 
-CUTS = ((0, 40), (40, PACK))
-
-
-def gather_kernel(x_ref, c_ref, rule_ref, rw_ref, cols_ref, count_ref,
+def far(way, ch):
+    return ch // (NCH // 2) == way
+
+
+CUTS = (0, 40, 72)
+NCH = len(CUTS) - 1
+
+
+def gather_kernel(x_hbm, c_hbm, rule_hbm, rw_hbm, cols_hbm, count_ref,
                   li_ref, lj_ref, p_ref, q_ref, table_ref, w_ref,
-                  b_ref, bi_ref, bj_ref, ring_send, ring_recv, side_send, side_recv):
+                  b_ref, bi_ref, bj_ref, x_ref, c_ref, rule_ref, cols_ref, rw_ref,
+                  ring_send, ring_recv, side_send, side_recv, load_sem):
     ring, z, core = place()
+    loads = [pltpu.make_async_copy(src, dst, load_sem.at[n]) for n, (src, dst) in enumerate((
+        (rule_hbm, rule_ref), (rw_hbm, rw_ref), (x_hbm, x_ref), (c_hbm, c_ref), (cols_hbm, cols_ref)))]
+    for cp in loads:
+        cp.start()
     barrier = pltpu.get_barrier_semaphore()
     peers = partners(ring, z, core)
     for peer in peers:
         pl.semaphore_signal(barrier, inc=1, device_id=peer, device_id_type=MESH)
 
+    for cp in loads:
+        cp.wait()
     rule = rule_ref[...]
     w = jnp.zeros((1, 512), jnp.float32)
     for r in range(RULES):
@@ -106,12 +118,12 @@
 
     def hop(way, h, ch):
         owner = owner_of(way, h)
-        rows = pl.ds(CUTS[ch][0], CUTS[ch][1] - CUTS[ch][0])
+        rows = pl.ds(CUTS[ch], CUTS[ch + 1] - CUTS[ch])
         src = b_ref.at[rows] if h == 0 else bi_ref.at[owner, rows]
         return remote(src, bi_ref.at[owner, rows], ring_send.at[way, h, ch], ring_recv.at[way, h, ch],
                       device(ring, z + 1 - 2 * way, core))
 
-    for ch in range(2):
+    for ch in range(NCH):
         for way in range(2):
             launch(hop(way, 0, ch))
     for n, (d, c) in enumerate(((1, 0), (1, 1), (2, 0), (2, 1))):
@@ -143,10 +155,10 @@
     expand_i(b_ref, z)
     expand_j(b_ref, core)
     for h in range(1, HOPS):
-        for ch in range(2):
+        for ch in range(NCH):
             for way in range(2):
                 hop(way, h - 1, ch).wait_recv()
-                if h < HOPS - 1 or ch == way:
+                if h < HOPS - 1 or far(way, ch):
                     launch(hop(way, h, ch))
         for way in range(2):
             k = owner_of(way, h)
@@ -157,7 +169,9 @@
                    device(ring, z, 1 - core)).wait_recv()
             expand_j(bj_ref.at[k], k)
     for way in range(2):
-        hop(way, HOPS - 1, way).wait_recv()
+        for ch in range(NCH):
+            if far(way, ch):
+                hop(way, HOPS - 1, ch).wait_recv()
     k = (z + HOPS) % RING_LEN
     expand_i(bi_ref.at[k], k)
     for cp in started:
@@ -173,10 +187,12 @@
         gather_kernel,
         out_shape=(s((16, 128, 512), b), s((12, 128, 512), b), s((16, 3, 256, 128), f), s((12, 8, 256), f),
                    s((16, 128), jnp.int32), s((8, 512), f)),
-        in_specs=[VM, VM, VM, SM, VM, SM],
+        in_specs=[HBM] * 5 + [pl.BlockSpec(memory_space=pltpu.SMEM)],
         out_specs=(VM,) * 6,
         scratch_shapes=[pltpu.VMEM((PACK, 512), f), pltpu.VMEM((8, PACK, 512), f), pltpu.VMEM((6, PACK, 512), f),
-                        dma((2, HOPS, 2)), dma((2, HOPS, 2)), dma((5,)), dma((6,))],
+                        pltpu.VMEM((64, 512), f), pltpu.VMEM((3, 512), f), pltpu.VMEM((1, 512), jnp.int32),
+                        pltpu.VMEM((1, SLOTS), jnp.int32), pltpu.SMEM((RULES,), f),
+                        dma((2, HOPS, NCH)), dma((2, HOPS, NCH)), dma((5,)), dma((6,)), dma((5,))],
         compiler_params=pltpu.CompilerParams(collective_id=0, has_side_effects=True, vmem_limit_bytes=20 << 20),
     )(x, coords, rule, rw, cols, count)
 
@@ -285,6 +301,14 @@
     )(li, lj, p, q, table)
 
 
+PARTS = 4
+SPAN = 64 // PARTS
+
+
+def near(way, ch):
+    return ch // (PARTS // 2) == way
+
+
 def reduce_kernel(yi_ref, yj_ref, w_ref, out_ref, flow, side, ring_send, ring_recv, side_send, side_recv):
     ring, z, core = place()
     barrier = pltpu.get_barrier_semaphore()
@@ -295,7 +319,7 @@
     started = []
 
     def part(ref, first, ch):
-        return ref.at[pl.ds(first, 2), pl.ds(32 * ch, 32)]
+        return ref.at[pl.ds(first, 2), pl.ds(SPAN * ch, SPAN)]
 
     def hop(way, h, ch, src):
         return remote(src, part(flow.at[way, h], 0, ch), ring_send.at[way, h, ch], ring_recv.at[way, h, ch],
@@ -308,10 +332,14 @@
         cp.start()
         started.append(cp)
 
-    for way in range(2):
-        launch(hop(way, 0, way, part(yi_ref, 2 * target(way, 0), way)))
-    for way in range(2):
-        launch(hop(way, 1, 1 - way, part(yi_ref, 2 * target(way, 1), 1 - way)))
+    for ch in range(PARTS):
+        for way in range(2):
+            if near(way, ch):
+                launch(hop(way, 0, ch, part(yi_ref, 2 * target(way, 0), ch)))
+    for ch in range(PARTS):
+        for way in range(2):
+            if not near(way, ch):
+                launch(hop(way, 1, ch, part(yi_ref, 2 * target(way, 1), ch)))
     n = 0
     for d in (1, 2):
         for c in range(2):
@@ -321,18 +349,18 @@
     launch(remote(yj_ref.at[pl.ds((1 - core) * 2, 2)], side.at[4], side_send.at[4], side_recv.at[4],
                   device(ring, z, 1 - core)))
     for h in range(1, HOPS):
-        for k in range(2):
-            for way in range(2):
-                ch = way if k == 0 else 1 - way
-                if k == 1 and h == 1:
-                    continue
-                here = part(flow.at[way, h - 1], 0, ch)
-                hop(way, h - 1, ch, here).wait_recv()
-                rows = slice(32 * ch, 32 * ch + 32)
-                flow[way, h - 1, :, rows, :] += yi_ref[pl.ds(2 * target(way, h), 2), rows, :]
-                launch(hop(way, h, ch, here))
+        for first in (False, True):
+            for ch in range(PARTS):
+                for way in range(2):
+                    if near(way, ch) != first or (h == 1 and not first):
+                        continue
+                    here = part(flow.at[way, h - 1], 0, ch)
+                    hop(way, h - 1, ch, here).wait_recv()
+                    rows = slice(SPAN * ch, SPAN * ch + SPAN)
+                    flow[way, h - 1, :, rows, :] += yi_ref[pl.ds(2 * target(way, h), 2), rows, :]
+                    launch(hop(way, h, ch, here))
     for way in range(2):
-        for ch in range(2):
+        for ch in range(PARTS):
             hop(way, HOPS - 1, ch, part(flow.at[way, 0], 0, ch)).wait_recv()
     for s in range(5):
         remote(side.at[s], side.at[s], side_send.at[s], side_recv.at[s], device(ring, z, 1 - core)).wait_recv()
@@ -353,14 +381,15 @@
         out_shape=jax.ShapeDtypeStruct((64, 512), f),
         in_specs=[VM] * 3, out_specs=VM,
         scratch_shapes=[pltpu.VMEM((2, HOPS, 2, 64, 256), f), pltpu.VMEM((5, 2, 64, 256), f),
-                        dma((2, HOPS, 2)), dma((2, HOPS, 2)), dma((5,)), dma((5,))],
+                        dma((2, HOPS, PARTS)), dma((2, HOPS, PARTS)), dma((5,)), dma((5,))],
         compiler_params=pltpu.CompilerParams(collective_id=1, has_side_effects=True, vmem_limit_bytes=16 << 20),
     )(yi, yj, w)
 
 
 def body(drive, coords, rule_index, rule_weight, pair_cols, pair_count):
-    li, lj, p, q, table, w = gather(drive.reshape(64, 512), coords, rule_index.reshape(1, 512), rule_weight,
-                                    pair_cols.reshape(1, SLOTS), pair_count)
+    held = [pltpu.with_memory_space_constraint(v, pltpu.HBM) for v in (
+        drive.reshape(64, 512), coords, rule_index.reshape(1, 512), rule_weight, pair_cols.reshape(1, SLOTS))]
+    li, lj, p, q, table, w = gather(*held, pair_count)
     yi, yj = compute(li, lj, p, q, table)
     return reduce(yi, yj, w).reshape(2, 32, 512)
 

time: 78.6 us -> 71.8 us (0.913)
  local copies, waits for them, and re-layouts: 4.24 us -> 0.66 us
  Pallas kernels: 73 us -> 69.8 us
    unnamed x11 -> x1, local copies, waits for them, and re-layouts: 4.24 us -> 0.66 us
    pallas_call x1, Pallas kernels: 28.6 us -> 25.8 us  [reduce(): pl.pallas_call(reduce_kernel, out_shape=jax.ShapeDtypeStruct((64, 512), f...]
where the time goes in v3:
time: 71.8 us; the launch traced here: 71.1 us
  Pallas kernels  69.8 us (97%)
    pallas_call x1, Pallas kernels, reduce(): pl.pallas_call(reduce_kernel, out_shape=jax.ShapeDtypeStruct((64, 512), f...  25.8 us
    pallas_call x1, Pallas kernels, gather(): pl.pallas_call(gather_kernel, out_shape=(s((16, 128, 512), b), s((12, 128...  25.6 us
    pallas_call x1, Pallas kernels, compute(): pl.pallas_call(compute_kernel, out_shape=(jax.ShapeDtypeStruct((16, 64, 2...  18.5 us

profile of v3, /device:TPU:1, one launch (start us, length us, event | category | flops | bytes accessed | tf_op | source)
XLA Modules:
  0.0 71.1 jit_solution(258530526418788029)
XLA Ops:
  0.7 25.6 %shard_map.64 = (bf16[16,128,512]{2,1,0:T(8,128)(2,1)S(1)}, bf16[12,128,512]{2,1,0:T(8,128)(2,1)S(1)}, f32[16,3,256,128]{3,2,1,0:T(8,128)S(1)}, f32[12,8,256]{2,...) custom-call(f32[64,512]{1,0:T(8,128)} %bitcast.5, f32[3,512]{1,0:T(4,128)} %c_hbm.1, s32[1,512]{1,0:T(1,128)} %bitcast.6, ...), custom_call_target="tpu_custom_call" | custom-call | tf_op jit(solution)/shard_map/pallas_call | solution.py:186
  26.2 18.5 %shard_map.65 = (f32[16,64,256]{2,1,0:T(8,128)S(1)}, f32[12,64,256]{2,1,0:T(8,128)S(1)}) custom-call(bf16[16,128,512]{2,1,0:T(8,128)(2,1)S(1)} %get-tuple-element.13.li, bf16[12,128,512]{2,1,0:T(8,128)(2,1)S(1)} %get-tuple-element.14.lj, f32[16,3,256,128]{3,2,1,0:T(8,128)S(1)} %get-tuple-element.15.p, f32[12,8,256]{2,1,0:T(8,128)S(1)} %get-tuple-element.16.q, ...), custom_call_target="tpu_custom_call" | custom-call | tf_op jit(solution)/shard_map/pallas_call | solution.py:292
  44.7 25.8 %shard_map.66 = f32[64,512]{1,0:T(8,128)S(1)} custom-call(f32[16,64,256]{2,1,0:T(8,128)S(1)} %get-tuple-element.18.yi_ref, f32[12,64,256]{2,1,0:T(8,128)S(1)} %get-tuple-element.19.yj_ref, f32[8,512]{1,0:T(8,128)S(1)} %get-tuple-element.20.w_ref), custom_call_target="tpu_custom_call" | custom-call | tf_op jit(solution)/shard_map/pallas_call | solution.py:379
  70.5 0.7 copy.9
